TPU v7x, 128 devices: a whole 4x4x4 slice. The times are simulated.
128 devices in a mesh: node: 32 (over z, y_lo, x), rep: 4 (over y_hi, core).
Axes of the slice: x: 4, y: 4 (y_hi: 2, y_lo: 2; y = y_hi * 2 + y_lo), z: 4, core: 2. Of those that a mesh axis runs over, the one named last changes fastest.
Arguments:
- node_feats: bfloat16 [65536, 256], P('node'), may hold values from -6 to 6
- weight: bfloat16 [256, 256], replicated, may hold values from -0.375 to 0.375
- cotangent: bfloat16 [65536, 256], P(('node', 'rep')), may hold values from -6 to 6
- tiles: bfloat16 [32, 4, 160, 256, 256], P('node', 'rep'), may hold values from -0.049804688 to 0.049804688
- tile_rows: int32 [32, 4, 160], P('node', 'rep'), may hold values from 0 to 7
- tile_cols: int32 [32, 4, 160], P('node', 'rep'), may hold values from 0 to 63
- tile_count: int32 [32, 4], P('node', 'rep'), may hold values from 80 to 160, as said below
Outputs:
- activated: bfloat16 [65536, 256], P(('node', 'rep'))
- feature_grad: bfloat16 [65536, 256], P(('node', 'rep'))
- weight_grad: float32 [256, 256], replicated
Inputs may be any that keep to these rules, and one draw needn't show every extreme that they name: `tile_count`: slots at and beyond a device's count are ignored; some device has all 160 slots live in every draw.
All inputs are finite; a program needn't handle non-finite values.
Results may differ from a plain program's by a relative error of at most 0.007.
Values may be sent and summed in bfloat16 or wider, within the bound.
No kernel may reach another device: no remote copies, remote signals or barrier semaphores. Data moves between devices by JAX's collectives and lax.ppermute only.
A program may use at most 256 MiB of HBM per device.

v0:
```python
import jax
import jax.numpy as jnp
from jax import lax
from jax.sharding import PartitionSpec as P


def body(node_feats, weight, cotangent, tiles, tile_rows, tile_cols, tile_count):
    nrep = lax.axis_size("rep")
    nnode = lax.axis_size("node")
    rep_idx = lax.axis_index("rep")
    rows, feat = node_feats.shape
    block = tiles.shape[-1]
    row_blocks = rows // block
    quarter = row_blocks // nrep
    share = rows // nrep
    compact_cols = quarter * nnode
    slot_tiles = tiles[0, 0]
    slot_rows = tile_rows[0, 0]
    slot_cols = tile_cols[0, 0]
    slot_total = slot_tiles.shape[0]
    live = jnp.arange(slot_total, dtype=jnp.int32) < tile_count[0, 0]
    live_scale = live.astype(jnp.float32)[:, None, None]
    feat_blocks = node_feats.reshape(row_blocks, block, feat)
    mine = lax.dynamic_slice_in_dim(feat_blocks, rep_idx * quarter, quarter, 0)
    compact = lax.all_gather(mine, "node", axis=0, tiled=True)
    picked = compact[slot_cols]
    forward_prod = (
        jnp.einsum("tab,tbf->taf", slot_tiles, picked, preferred_element_type=jnp.float32)
        * live_scale
    )
    partial_agg = (
        jnp.zeros((row_blocks, block, feat), jnp.float32)
        .at[slot_rows]
        .add(forward_prod)
        .reshape(rows, feat)
    )
    scale = float(rows * nnode) ** (-0.5)
    aggregated = lax.psum(partial_agg, "rep").astype(jnp.bfloat16)
    cot_full = lax.all_gather(cotangent, "rep", axis=0, tiled=True)
    pre = jnp.dot(aggregated, weight, preferred_element_type=jnp.float32)
    sig = jax.nn.sigmoid(pre)
    activated_full = (pre * sig).astype(jnp.bfloat16)
    dpre = (cot_full.astype(jnp.float32) * sig * (1.0 + pre * (1.0 - sig))).astype(jnp.bfloat16)
    dagg = jnp.dot(dpre, weight.T, preferred_element_type=jnp.float32).astype(jnp.bfloat16)
    activated = lax.dynamic_slice_in_dim(activated_full, rep_idx * share, share, 0)
    agg_share = lax.dynamic_slice_in_dim(aggregated, rep_idx * share, share, 0)
    dpre_share = lax.dynamic_slice_in_dim(dpre, rep_idx * share, share, 0)
    weight_term = lax.dot_general(
        agg_share, dpre_share, (((0,), (0,)), ((), ())), preferred_element_type=jnp.float32
    )
    weight_grad = lax.psum(weight_term, ("node", "rep")) * scale
    dagg_blocks = dagg.reshape(row_blocks, block, feat)
    backward_prod = (
        jnp.einsum(
            "tab,taf->tbf", slot_tiles, dagg_blocks[slot_rows], preferred_element_type=jnp.float32
        )
        * live_scale
    )
    column_part = (
        jnp.zeros((compact_cols, block, feat), jnp.float32).at[slot_cols].add(backward_prod)
    )
    owned = lax.psum_scatter(column_part, "node", scatter_dimension=0, tiled=True)
    feature_grad = owned.reshape(quarter * block, feat).astype(jnp.bfloat16)
    return (activated, feature_grad, weight_grad)


def solution(mesh):
    placed = (
        P("node", None),
        P(),
        P(("node", "rep"), None),
        P("node", "rep", None, None, None),
        P("node", "rep", None),
        P("node", "rep", None),
        P("node", "rep"),
    )
    return jax.shard_map(
        body,
        mesh=mesh,
        in_specs=placed,
        out_specs=(P(("node", "rep"), None), P(("node", "rep"), None), P()),
        check_vma=False,
    )
```

profile of v0, /device:TPU:0, one launch (start us, length us, event | category | flops | bytes accessed | tf_op | source)
XLA Modules:
  0.0 760.6 jit_solution(5284792371590088112)
XLA Ops:
  7.2 0.0 copy-start
  7.2 0.0 all-gather.3.cloned.1.call-start
  7.2 1.2 copy-done
  8.4 0.7 constant_dynamic-slice_fusion
  9.1 0.0 all-gather.3.cloned.1.call-update
  9.1 0.0 all-gather.5.cloned.1.call-start
  9.2 0.7 all-gather.5.cloned.1.call-update
  9.9 0.0 all-reduce.3.cloned.1.call-start
  9.9 0.7 compare_select_fusion
  10.6 0.0 copy-start.4
  11.3 0.7 compare_select_fusion.1
  12.0 167.9 %all-gather.3.cloned.1.call-done = bf16[64,256,256]{2,1,0:T(8,128)(2,1)} async-done(((bf16[2,256,256]{2,1,0:T(8,128)(2,1)}), bf16[64,256,256]{2,1,0:T(8,128)(2,1)}) %all-gather.3.cloned.1.call-update) | async-done | bytes 8388624 | tf_op jit(solution)/shard_map/all_gather | solution.py:25
  179.9 13.0 %gather_fusion = bf16[160,256,256]{2,1,0:T(8,128)(2,1)} fusion(bf16[64,256,256]{2,1,0:T(8,128)(2,1)} %all-gather.3.cloned.1.call-done, s32[1024]{0:T(1024)S(1)} %pad_clamp_fusion.1), kind=kCustom, calls=%fused_computation | custom fusion | bytes 41943680 | tf_op jit(solution)/shard_map/gather | solution.py:26
  192.9 0.0 copy-done.4
  192.9 30.3 %multiply_bitcast_fusion.1 = f32[160,256,256]{1,2,0:T(8,128)} fusion(f32[160]{0:T(256)S(1)} %compare_convert_fusion, bf16[160,256,256]{2,1,0:T(8,128)(2,1)} %gather_fusion, bf16[1,1,160,256,256]{4,3,2,1,0:T(8,128)(2,1)} %param.10), kind=kOutput, calls=%fused_computation.5 | convolution fusion | flops 5379194880 | bytes 83886720 | tf_op jit(solution)/shard_map/tab,tbf->taf/dot_general | solution.py:28
  223.2 41.6 %copy.17 = f32[160,256,256]{2,1,0:T(8,128)} copy(f32[160,256,256]{1,2,0:T(8,128)} %multiply_bitcast_fusion.1) | data formatting | bytes 83886080 | tf_op jit(solution)/shard_map/mul | solution.py:28
  264.8 0.2 broadcast_in_dim.4
  265.0 0.0 copy-start.3
  265.0 56.7 %scatter_fusion = f32[8,256,256]{2,1,0:T(8,128)S(1)} fusion(f32[8,256,256]{2,1,0:T(8,128)S(1)} %broadcast_in_dim.4, s32[160]{0:T(256)S(1)} %bitcast.38, f32[160,256,256]{2,1,0:T(8,128)} %copy.17), kind=kCustom, calls=%fused_computation.2 | custom fusion | flops 10485760 | bytes 125829760 | tf_op jit(solution)/shard_map/scatter-add | solution.py:34
  321.7 42.3 %all-reduce.4 = bf16[2048,256]{1,0:T(8,128)(2,1)S(1)} all-reduce(f32[2048,256]{1,0:T(8,128)S(1)} %bitcast.32), channel_id=1, replica_groups=mesh['node'=32,'rep'=4] {'rep'}, use_global_device_ids=true, to_apply=%region_1.0 | all-reduce | flops 524288 | bytes 3145728 | tf_op jit(solution)/shard_map/psum | solution.py:38
  364.0 0.0 copy-start.2
  364.0 0.0 all-gather.5.cloned.1.call-done
  364.1 0.0 copy-done.3
  364.1 3.8 multiply_convert_fusion
  367.8 0.0 copy-done.2
  367.8 0.5 convolution_convert_fusion
  368.3 1.9 fusion.9
  370.2 0.0 all-reduce.3.cloned.1.call-update
  370.3 0.2 reduce-scatter.2.cloned.1.call-start
  370.5 9.6 %gather_fusion.1 = bf16[160,256,256]{2,1,0:T(8,128)(2,1)} fusion(bf16[8,256,256]{2,1,0:T(8,128)(2,1)S(1)} %bitcast.33, s32[1024]{0:T(1024)S(1)} %pad_clamp_fusion), kind=kCustom, calls=%fused_computation.1 | custom fusion | bytes 41943680 | tf_op jit(solution)/shard_map/gather | solution.py:55
  380.1 26.6 %multiply_bitcast_fusion = f32[160,256,256]{1,2,0:T(8,128)} fusion(f32[160]{0:T(256)S(1)} %compare_convert_fusion, bf16[160,256,256]{2,1,0:T(8,128)(2,1)} %gather_fusion.1, bf16[1,1,160,256,256]{4,3,2,1,0:T(8,128)(2,1)} %param.10), kind=kOutput, calls=%fused_computation.4 | convolution fusion | flops 5379194880 | bytes 83886720 | tf_op jit(solution)/shard_map/tab,taf->tbf/dot_general | solution.py:54
  406.7 0.0 copy-start.5
  406.7 41.7 %copy.19 = f32[160,256,256]{2,1,0:T(8,128)} copy(f32[160,256,256]{1,2,0:T(8,128)} %multiply_bitcast_fusion) | data formatting | bytes 83886080 | tf_op jit(solution)/shard_map/mul | solution.py:54
  448.3 7.8 %broadcast_in_dim.5 = f32[64,256,256]{2,1,0:T(8,128)} broadcast(f32[]{:T(128)} %constant.10.clone.1), dimensions={} | broadcast | bytes 16777220 | tf_op jit(solution)/shard_map/broadcast_in_dim | solution.py:60
  456.1 0.0 copy-done.5
  456.1 0.0 copy-start.1
  456.1 91.3 %scatter_fusion.1 = f32[64,256,256]{2,1,0:T(8,128)} fusion(f32[64,256,256]{2,1,0:T(8,128)} %broadcast_in_dim.5, s32[160]{0:T(256)S(1)} %bitcast.36, f32[160,256,256]{2,1,0:T(8,128)} %copy.19), kind=kCustom, calls=%fused_computation.3 | custom fusion | flops 10485760 | bytes 125829760 | tf_op jit(solution)/shard_map/scatter-add | solution.py:60
  547.4 0.0 reduce-scatter.2.cloned.1.call-update
  547.5 1.8 fusion.8
  549.3 0.0 all-reduce.3.cloned.1.call-done
  549.3 1.7 broadcast_multiply_fusion
  550.9 201.3 %reduce-scatter.2.cloned.1.call-done = f32[2,256,256]{2,1,0:T(8,128)} async-done(((f32[64,256,256]{2,1,0:T(8,128)}), f32[2,256,256]{2,1,0:T(8,128)}) %reduce-scatter.2.cloned.1.call-update) | async-done | bytes 524304 | tf_op jit(solution)/shard_map/reduce_scatter | solution.py:62
  752.3 1.8 convert_element_type.34
  754.0 0.0 copy-done.1
  (3 shorter events, 0.0 us)
Async XLA Ops:
  7.2 1.2 copy-start
  7.2 172.7 %all-gather.3.cloned.1.call-start = ((), (), s32[]{:S(2)}) async-start(), calls=%async_computation.1 | async-start | bytes 8650752 | tf_op jit(solution)/shard_map/all_gather | solution.py:25
  9.1 354.9 %all-gather.5.cloned.1.call-start = ((), (), s32[]{:S(2)}) async-start(), calls=%async_computation.2 | async-start | bytes 1310720 | tf_op jit(solution)/shard_map/all_gather | solution.py:39
  9.9 539.4 %all-reduce.3.cloned.1.call-start = ((), (), s32[]{:S(2)}) async-start(), calls=%async_computation.4 | async-start | bytes 524288 | tf_op jit(solution)/shard_map/psum | solution.py:51
  10.6 182.3 %copy-start.4 = (s32[160,1]{0,1:T(1,128)}, s32[160,1]{0,1:T(1,128)S(1)}, u32[]{:S(2)}) copy-start(s32[160,1]{0,1:T(1,128)S(1)} %compare_select_fusion) | copy-start | bytes 1924
  265.0 99.0 %copy-start.3 = (bf16[256,256]{1,0:T(8,128)(2,1)S(1)}, bf16[256,256]{1,0:T(8,128)(2,1)}, u32[]{:S(2)}) copy-start(bf16[256,256]{1,0:T(8,128)(2,1)} %param.8) | copy-start | bytes 393220
  364.0 3.8 copy-start.2
  370.3 382.0 %reduce-scatter.2.cloned.1.call-start = ((), (), s32[]{:S(2)}) async-start(), calls=%async_computation.3 | async-start | bytes 17301504 | tf_op jit(solution)/shard_map/reduce_scatter | solution.py:62
  406.7 49.5 %copy-start.5 = (s32[160,1]{0,1:T(1,128)S(1)}, s32[160,1]{0,1:T(1,128)}, u32[]{:S(2)}) copy-start(s32[160,1]{0,1:T(1,128)} %copy-done.4) | copy-start | bytes 1924
  456.1 297.9 %copy-start.1 = (bf16[2048,256]{1,0:T(8,128)(2,1)S(1)}, bf16[2048,256]{1,0:T(8,128)(2,1)}, u32[]{:S(2)}) copy-start(bf16[2048,256]{1,0:T(8,128)(2,1)} %param.7) | copy-start | bytes 3145732
Sparse Core Ops, SparseCore 0:
  10.2 169.6 all-gather.2
  181.6 21.7 all-gather.4
  370.4 142.5 all-reduce.2
  547.6 204.6 reduce-scatter.1
where the time goes:
time: 763 us; the launch traced here: 761 us
  waiting for transfers between devices  370 us (48%)
  other arithmetic  155 us (20%)
  local copies, waits for them, and re-layouts  116 us (15%)
  matrix products  63 us (8%)
  blocking collectives  42.3 us (6%)
  between operations  14.5 us (2%)
    reduce_scatter x1, waiting for transfers between devices, body(): lax.psum_scatter(column_part, 'node', scatter_dimension=0, tiled=True)  201 us
    all_gather x1, waiting for transfers between devices, body(): compact = lax.all_gather(mine, 'node', axis=0, tiled=True)  168 us
    scatter-add x1, other arithmetic, body(): jnp.zeros((compact_cols, block, feat), jnp.float32).at[slot_cols]  91.3 us
    scatter-add x1, other arithmetic, body(): partial_agg = jnp.zeros((row_blocks, block, feat), jnp.float32).at[slot_r...  56.7 us
    psum x1, blocking collectives, body(): aggregated = lax.psum(partial_agg, 'rep').astype(jnp.bfloat16)  42.3 us
    mul x1, local copies, waits for them, and re-layouts, body(): jnp.einsum('tab,taf->tbf', slot_tiles, dagg_blocks[slot_rows], preferred_...  41.7 us
    mul x1, local copies, waits for them, and re-layouts, body(): jnp.einsum('tab,tbf->taf', slot_tiles, picked, preferred_element_type=jnp...  41.6 us
    dot_general x1, matrix products, body(): jnp.einsum('tab,tbf->taf', slot_tiles, picked, preferred_element_type=jnp...  30.3 us
  transfers between devices with their start and end apart: 4, of which 2 were waited for; matrix products, arithmetic and copies ran while one was open for 43% of the time, Pallas kernels for 0%

commit v1 on v0

--- a/solution.py
+++ b/solution.py
@@ -22,7 +22,9 @@
     live_scale = live.astype(jnp.float32)[:, None, None]
     feat_blocks = node_feats.reshape(row_blocks, block, feat)
     mine = lax.dynamic_slice_in_dim(feat_blocks, rep_idx * quarter, quarter, 0)
-    compact = lax.all_gather(mine, "node", axis=0, tiled=True)
+    compact = jnp.concatenate(
+        lax.all_to_all(jnp.stack([mine] * lax.axis_size("node")), "node", 0, 0), axis=0
+    )
     picked = compact[slot_cols]
     forward_prod = (
         jnp.einsum("tab,tbf->taf", slot_tiles, picked, preferred_element_type=jnp.float32)

time: 763 us -> 728 us (0.954)
  waiting for transfers between devices: 370 us -> 323 us
  starting transfers between devices: 0.34 us -> 9.69 us
    all_gather x1 -> x0, waiting for transfers between devices: 168 us -> none  [body(): compact = lax.all_gather(mine, 'node', axis=0, tiled=True)]
    all_to_all x0 -> x1, waiting for transfers between devices: none -> 123 us  [body(): lax.all_to_all(jnp.stack([mine] * lax.axis_size('node')), 'node', 0, 0)]
    all_to_all x0 -> x1, starting transfers between devices: none -> 9.39 us  [body(): lax.all_to_all(jnp.stack([mine] * lax.axis_size('node')), 'node', 0, 0)]
  transfers between devices with their start and end apart: 4 -> 4, of which waited for: 2 -> 2; matrix products, arithmetic and copies ran while one was open for 43% -> 44% of each run, Pallas kernels for 0% -> 0%
where the time goes in v1:
time: 728 us; the launch traced here: 725 us
  waiting for transfers between devices  323 us (44%)
  other arithmetic  153 us (21%)
  local copies, waits for them, and re-layouts  119 us (16%)
  matrix products  63.1 us (9%)
  blocking collectives  42.7 us (6%)
  between operations  14.6 us (2%)
  starting transfers between devices  9.69 us (1%)
    reduce_scatter x1, waiting for transfers between devices, body(): lax.psum_scatter(column_part, 'node', scatter_dimension=0, tiled=True)  199 us
    all_to_all x1, waiting for transfers between devices, body(): lax.all_to_all(jnp.stack([mine] * lax.axis_size('node')), 'node', 0, 0)  123 us
    scatter-add x1, other arithmetic, body(): jnp.zeros((compact_cols, block, feat), jnp.float32).at[slot_cols]  91.2 us
    scatter-add x1, other arithmetic, body(): partial_agg = jnp.zeros((row_blocks, block, feat), jnp.float32).at[slot_r...  56.7 us
    psum x1, blocking collectives, body(): aggregated = lax.psum(partial_agg, 'rep').astype(jnp.bfloat16)  42.7 us
    mul x1, local copies, waits for them, and re-layouts, body(): jnp.einsum('tab,taf->tbf', slot_tiles, dagg_blocks[slot_rows], preferred_...  41.7 us
    mul x1, local copies, waits for them, and re-layouts, body(): jnp.einsum('tab,tbf->taf', slot_tiles, picked, preferred_element_type=jnp...  41.6 us
    dot_general x1, matrix products, body(): jnp.einsum('tab,tbf->taf', slot_tiles, picked, preferred_element_type=jnp...  30.3 us
  transfers between devices with their start and end apart: 4, of which 2 were waited for; matrix products, arithmetic and copies ran while one was open for 44% of the time, Pallas kernels for 0%

profile of v1, /device:TPU:0, one launch (start us, length us, event | category | flops | bytes accessed | tf_op | source)
XLA Modules:
  0.0 725.4 jit_solution(5454022224339401305)
XLA Ops:
  7.2 0.0 copy-start
  7.2 0.0 copy-start.7
  7.2 0.0 copy-start.6
  7.2 1.2 copy-done
  8.4 4.2 stack.2
  12.7 9.4 %all-to-all-start = ((bf16[32,2,256,256]{3,2,1,0:T(8,128)(2,1)}), bf16[32,2,256,256]{3,2,1,0:T(8,128)(2,1)}, u32[]{:S(2)}, u32[]{:S(2)}) async-start(bf16[32,2,256,256]{3,2,1,0:T(8,128)(2,1)} %stack.2), calls=%async_computation | async-start | bytes 16777216 | tf_op jit(solution)/shard_map/all_to_all | solution.py:26
  22.1 0.0 all-gather.2.cloned.1.call-start
  22.1 0.7 all-gather.2.cloned.1.call-update
  22.8 0.0 all-reduce.3.cloned.1.call-start
  23.5 0.0 copy-done.7
  23.5 0.0 copy-done.6
  23.5 0.0 copy-start.4
  23.6 123.0 %all-to-all-done = bf16[32,2,256,256]{3,2,1,0:T(8,128)(2,1)} async-done(((bf16[32,2,256,256]{3,2,1,0:T(8,128)(2,1)}), bf16[32,2,256,256]{3,2,1,0:T(8,128)(2,1)}, u32[]{:S(2)}, u32[]{:S(2)}) %all-to-all-start) | async-done | bytes 8388640 | tf_op jit(solution)/shard_map/all_to_all | solution.py:26
  146.6 13.0 %gather_fusion = bf16[160,256,256]{2,1,0:T(8,128)(2,1)} fusion(bf16[64,256,256]{2,1,0:T(8,128)(2,1)} %bitcast.3, s32[1024]{0:T(1024)S(1)} %pad_clamp_fusion.1), kind=kCustom, calls=%fused_computation | custom fusion | bytes 41943680 | tf_op jit(solution)/shard_map/gather | solution.py:28
  159.6 0.0 copy-done.4
  159.6 30.3 %multiply_bitcast_fusion.1 = f32[160,256,256]{1,2,0:T(8,128)} fusion(f32[160]{0:T(256)S(1)} %compare_convert_fusion, bf16[160,256,256]{2,1,0:T(8,128)(2,1)} %gather_fusion, bf16[1,1,160,256,256]{4,3,2,1,0:T(8,128)(2,1)} %param.10), kind=kOutput, calls=%fused_computation.5 | convolution fusion | flops 5379194880 | bytes 83886720 | tf_op jit(solution)/shard_map/tab,tbf->taf/dot_general | solution.py:30
  189.9 41.6 %copy.13 = f32[160,256,256]{2,1,0:T(8,128)} copy(f32[160,256,256]{1,2,0:T(8,128)} %multiply_bitcast_fusion.1) | data formatting | bytes 83886080 | tf_op jit(solution)/shard_map/mul | solution.py:30
  231.5 0.2 broadcast_in_dim.4
  231.7 0.0 copy-start.3
  231.7 56.7 %scatter_fusion = f32[8,256,256]{2,1,0:T(8,128)S(1)} fusion(f32[8,256,256]{2,1,0:T(8,128)S(1)} %broadcast_in_dim.4, s32[160]{0:T(256)S(1)} %bitcast.39, f32[160,256,256]{2,1,0:T(8,128)} %copy.13), kind=kCustom, calls=%fused_computation.2 | custom fusion | flops 10485760 | bytes 125829760 | tf_op jit(solution)/shard_map/scatter-add | solution.py:36
  288.4 42.7 %all-reduce.4 = bf16[2048,256]{1,0:T(8,128)(2,1)S(1)} all-reduce(f32[2048,256]{1,0:T(8,128)S(1)} %bitcast.33), channel_id=1, replica_groups=mesh['node'=32,'rep'=4] {'rep'}, use_global_device_ids=true, to_apply=%region_1.0 | all-reduce | flops 524288 | bytes 3145728 | tf_op jit(solution)/shard_map/psum | solution.py:40
  331.1 0.0 copy-start.2
  331.1 0.0 all-gather.2.cloned.1.call-done
  331.1 0.0 copy-done.3
  331.1 3.8 multiply_convert_fusion
  334.9 0.0 copy-done.2
  334.9 0.5 convolution_convert_fusion
  335.4 1.9 fusion.9
  337.3 0.0 all-reduce.3.cloned.1.call-update
  337.3 0.2 reduce-scatter.2.cloned.1.call-start
  337.5 9.6 %gather_fusion.1 = bf16[160,256,256]{2,1,0:T(8,128)(2,1)} fusion(bf16[8,256,256]{2,1,0:T(8,128)(2,1)S(1)} %bitcast.34, s32[1024]{0:T(1024)S(1)} %pad_clamp_fusion), kind=kCustom, calls=%fused_computation.1 | custom fusion | bytes 41943680 | tf_op jit(solution)/shard_map/gather | solution.py:57
  347.1 26.6 %multiply_bitcast_fusion = f32[160,256,256]{1,2,0:T(8,128)} fusion(f32[160]{0:T(256)S(1)} %compare_convert_fusion, bf16[160,256,256]{2,1,0:T(8,128)(2,1)} %gather_fusion.1, bf16[1,1,160,256,256]{4,3,2,1,0:T(8,128)(2,1)} %param.10), kind=kOutput, calls=%fused_computation.4 | convolution fusion | flops 5379194880 | bytes 83886720 | tf_op jit(solution)/shard_map/tab,taf->tbf/dot_general | solution.py:56
  373.7 0.0 copy-start.5
  373.7 41.7 %copy.15 = f32[160,256,256]{2,1,0:T(8,128)} copy(f32[160,256,256]{1,2,0:T(8,128)} %multiply_bitcast_fusion) | data formatting | bytes 83886080 | tf_op jit(solution)/shard_map/mul | solution.py:56
  415.4 7.8 %broadcast_in_dim.5 = f32[64,256,256]{2,1,0:T(8,128)} broadcast(f32[]{:T(128)} %constant.10.clone.1), dimensions={} | broadcast | bytes 16777220 | tf_op jit(solution)/shard_map/broadcast_in_dim | solution.py:62
  423.2 0.0 copy-done.5
  423.2 0.0 copy-start.1
  423.2 91.2 %scatter_fusion.1 = f32[64,256,256]{2,1,0:T(8,128)} fusion(f32[64,256,256]{2,1,0:T(8,128)} %broadcast_in_dim.5, s32[160]{0:T(256)S(1)} %bitcast.37, f32[160,256,256]{2,1,0:T(8,128)} %copy.15), kind=kCustom, calls=%fused_computation.3 | custom fusion | flops 10485760 | bytes 125829760 | tf_op jit(solution)/shard_map/scatter-add | solution.py:62
  514.4 0.0 reduce-scatter.2.cloned.1.call-update
  514.4 1.8 fusion.8
  516.2 0.0 all-reduce.3.cloned.1.call-done
  516.2 1.7 broadcast_multiply_fusion
  517.9 199.1 %reduce-scatter.2.cloned.1.call-done = f32[2,256,256]{2,1,0:T(8,128)} async-done(((f32[64,256,256]{2,1,0:T(8,128)}), f32[2,256,256]{2,1,0:T(8,128)}) %reduce-scatter.2.cloned.1.call-update) | async-done | bytes 524304 | tf_op jit(solution)/shard_map/reduce_scatter | solution.py:64
  717.0 1.8 convert_element_type.34
  718.8 0.0 copy-done.1
  (5 shorter events, 0.0 us)
Async XLA Ops:
  7.2 1.2 copy-start
  7.2 16.3 %copy-start.7 = (s32[1,1,160]{2,1,0:T(1,128)S(1)}, s32[1,1,160]{2,1,0:T(1,128)}, u32[]{:S(2)}) copy-start(s32[1,1,160]{2,1,0:T(1,128)} %param.11) | copy-start | bytes 1924
  7.2 16.3 %copy-start.6 = (s32[1,1,160]{2,1,0:T(1,128)S(1)}, s32[1,1,160]{2,1,0:T(1,128)}, u32[]{:S(2)}) copy-start(s32[1,1,160]{2,1,0:T(1,128)} %param.12) | copy-start | bytes 1924
  12.7 133.9 %all-to-all-start = ((bf16[32,2,256,256]{3,2,1,0:T(8,128)(2,1)}), bf16[32,2,256,256]{3,2,1,0:T(8,128)(2,1)}, u32[]{:S(2)}, u32[]{:S(2)}) async-start(bf16[32,2,256,256]{3,2,1,0:T(8,128)(2,1)} %stack.2), calls=%async_computation | async-start | bytes 16777216 | tf_op jit(solution)/shard_map/all_to_all | solution.py:26
  22.1 309.0 %all-gather.2.cloned.1.call-start = ((), (), s32[]{:S(2)}) async-start(), calls=%async_computation.2 | async-start | bytes 1310720 | tf_op jit(solution)/shard_map/all_gather | solution.py:41
  22.8 493.4 %all-reduce.3.cloned.1.call-start = ((), (), s32[]{:S(2)}) async-start(), calls=%async_computation.4 | async-start | bytes 524288 | tf_op jit(solution)/shard_map/psum | solution.py:53
  23.5 136.1 %copy-start.4 = (s32[160,1]{0,1:T(1,128)}, s32[160,1]{0,1:T(1,128)S(1)}, u32[]{:S(2)}) copy-start(s32[160,1]{0,1:T(1,128)S(1)} %get-tuple-element.6) | copy-start | bytes 1924
  231.7 99.4 %copy-start.3 = (bf16[256,256]{1,0:T(8,128)(2,1)S(1)}, bf16[256,256]{1,0:T(8,128)(2,1)}, u32[]{:S(2)}) copy-start(bf16[256,256]{1,0:T(8,128)(2,1)} %param.8) | copy-start | bytes 393220
  331.1 3.8 copy-start.2
  337.3 379.7 %reduce-scatter.2.cloned.1.call-start = ((), (), s32[]{:S(2)}) async-start(), calls=%async_computation.3 | async-start | bytes 17301504 | tf_op jit(solution)/shard_map/reduce_scatter | solution.py:64
  373.7 49.5 %copy-start.5 = (s32[160,1]{0,1:T(1,128)S(1)}, s32[160,1]{0,1:T(1,128)}, u32[]{:S(2)}) copy-start(s32[160,1]{0,1:T(1,128)} %copy-done.4) | copy-start | bytes 1924
  423.2 295.6 %copy-start.1 = (bf16[2048,256]{1,0:T(8,128)(2,1)S(1)}, bf16[2048,256]{1,0:T(8,128)(2,1)}, u32[]{:S(2)}) copy-start(bf16[2048,256]{1,0:T(8,128)(2,1)} %param.7) | copy-start | bytes 3145732
Sparse Core Ops, SparseCore 0:
  24.6 58.2 all-gather.1
  337.4 140.1 all-reduce.2
  514.5 202.4 reduce-scatter.1
